TPU v7x, 32 devices: a whole 2x2x4 slice. The times are simulated.
32 devices in a mesh: gz: 16 (over z, x, core), gy: 2 (over y).
Axes of the slice: x: 2, y: 2, z: 4, core: 2. Of those that a mesh axis runs over, the one named last changes fastest.
Arguments:
- vorticity: float32 [256, 128, 512], P('gz', 'gy'), may hold values from -12 to 12
- keep_one: int32 [7, 128, 64, 256], P(None, 'gz', 'gy'), may hold values 0 or 1
- keep_two: int32 [7, 64, 32, 128], P(None, 'gz', 'gy'), may hold values 0 or 1
- keep_three: int32 [7, 32, 16, 64], P(None, 'gz', 'gy'), may hold values 0 or 1
- keep_four: int32 [7, 16, 8, 32], P(None, 'gz', 'gy'), may hold values 0 or 1
- keep_coarse: int32 [16, 8, 32], P('gz', 'gy'), may hold values 0 or 1
Outputs:
- coherent: float32 [256, 128, 512], P('gz', 'gy')
All inputs are finite; a program needn't handle non-finite values. No bound on the sum of `keep_one` or of `keep_two` or of `keep_three` or of `keep_four` or of `keep_coarse` on one device may be relied on, other than what follows from the above.
Results may differ from a plain program's by a relative error of at most 0.00017.
Values sent between devices are 32-bit elements; how exact they have to be, the bound alone decides.
A program may use at most 128 MiB of HBM per device.

v0:
```python
import jax
import jax.numpy as jnp
from jax import lax
from jax.sharding import PartitionSpec as P

low_taps = (
    0.11154074335008017,
    0.4946238903983854,
    0.7511339080215775,
    0.3152503517092432,
    -0.22626469396516913,
    -0.12976686756709563,
    0.09750160558707936,
    0.02752286553001629,
    -0.031582039318031156,
    0.0005538422009938016,
    0.004777257511010651,
    -0.00107730108499558,
)
high_taps = tuple(((-1.0) ** k * low_taps[11 - k] for k in range(12)))


def shifted(shard, axis, by):
    devices = lax.axis_size(axis)
    return lax.ppermute(shard, axis, [(i, (i + by) % devices) for i in range(devices)])


def split_pair(extended, axis_dim, length):
    low_part = None
    high_part = None
    for k in range(12):
        sliced = lax.slice_in_dim(extended, k, k + length - 1, stride=2, axis=axis_dim)
        if k == 0:
            low_part = low_taps[k] * sliced
            high_part = high_taps[k] * sliced
        else:
            low_part = low_part + low_taps[k] * sliced
            high_part = high_part + high_taps[k] * sliced
    return (low_part, high_part)


def merge_pair(low_ext, high_ext, axis_dim, coarse_len):
    even_part = None
    odd_part = None
    for t in range(6):
        low_slice = lax.slice_in_dim(low_ext, 5 - t, 5 - t + coarse_len, axis=axis_dim)
        high_slice = lax.slice_in_dim(high_ext, 5 - t, 5 - t + coarse_len, axis=axis_dim)
        even_term = low_taps[2 * t] * low_slice + high_taps[2 * t] * high_slice
        odd_term = low_taps[2 * t + 1] * low_slice + high_taps[2 * t + 1] * high_slice
        if t == 0:
            even_part = even_term
            odd_part = odd_term
        else:
            even_part = even_part + even_term
            odd_part = odd_part + odd_term
    paired = jnp.stack([even_part, odd_part], axis=axis_dim + 1)
    new_shape = even_part.shape[:axis_dim] + (2 * coarse_len,) + even_part.shape[axis_dim + 1 :]
    return paired.reshape(new_shape)


def split_rows(half_len, ext_len, taps):
    out_ids = jnp.arange(half_len, dtype=jnp.int32)[:, None]
    in_ids = jnp.arange(ext_len, dtype=jnp.int32)[None, :]
    offset = in_ids - 2 * out_ids
    matrix = jnp.zeros((half_len, ext_len), jnp.float32)
    for k in range(12):
        matrix = matrix + jnp.where(offset == k, taps[k], 0.0)
    return matrix


def merge_rows(coarse_len, taps):
    out_ids = jnp.arange(2 * coarse_len, dtype=jnp.int32)[:, None]
    in_ids = jnp.arange(coarse_len + 5, dtype=jnp.int32)[None, :]
    phase = out_ids % 2
    start = out_ids // 2
    matrix = jnp.zeros((2 * coarse_len, coarse_len + 5), jnp.float32)
    for t in range(6):
        hit_pos = in_ids == start + 5 - t
        matrix = matrix + jnp.where(hit_pos & (phase == 0), taps[2 * t], 0.0)
        matrix = matrix + jnp.where(hit_pos & (phase == 1), taps[2 * t + 1], 0.0)
    return matrix


def rows_product(source, matrix):
    return jnp.einsum(
        "...yx,ky->...kx",
        source,
        matrix,
        precision=lax.Precision.HIGHEST,
        preferred_element_type=jnp.float32,
    )


def x_matrix(x_len):
    row_ids = jnp.arange(x_len, dtype=jnp.int32)[:, None]
    col_ids = jnp.arange(x_len, dtype=jnp.int32)[None, :]
    half_len = x_len // 2
    col_pos = col_ids % half_len
    is_low = col_ids < half_len
    matrix = jnp.zeros((x_len, x_len), jnp.float32)
    for k in range(12):
        is_hit = (2 * col_pos + k) % x_len == row_ids
        matrix = matrix + jnp.where(is_hit, jnp.where(is_low, low_taps[k], high_taps[k]), 0.0)
    return matrix


def x_forward(source, matrix):
    return jnp.dot(
        source, matrix, precision=lax.Precision.HIGHEST, preferred_element_type=jnp.float32
    )


def x_inverse(source, matrix):
    return jnp.dot(
        source, matrix.T, precision=lax.Precision.HIGHEST, preferred_element_type=jnp.float32
    )


def fetch_rim(source, axis_dim, rim_width, forward, along_z):
    length = source.shape[axis_dim]
    hop_count = -(-rim_width // length)
    pieces = []
    for hop_no in range(1, hop_count + 1):
        take_len = min(length, rim_width - (hop_no - 1) * length)
        if forward:
            sliced = lax.slice_in_dim(source, 0, take_len, axis=axis_dim)
            offset = -hop_no
        else:
            sliced = lax.slice_in_dim(source, length - take_len, length, axis=axis_dim)
            offset = hop_no
        if along_z:
            received = shifted(sliced, "gz", offset)
        else:
            received = shifted(sliced, "gy", offset)
        pieces.append(received)
    if forward:
        return jnp.concatenate([source] + pieces, axis=axis_dim)
    return jnp.concatenate(pieces[::-1] + [source], axis=axis_dim)


def analyse_axis(source, axis_dim, stack_at, along_z):
    length = source.shape[axis_dim]
    extended = fetch_rim(source, axis_dim, 10, True, along_z)
    if along_z:
        low_part, high_part = split_pair(extended, axis_dim, length)
    else:
        ext_len = extended.shape[axis_dim]
        low_part = rows_product(extended, split_rows(length // 2, ext_len, low_taps))
        high_part = rows_product(extended, split_rows(length // 2, ext_len, high_taps))
    return jnp.stack([low_part, high_part], axis=stack_at)


def join_axis(paired, pair_axis, axis_dim, along_z):
    coarse_len = paired.shape[axis_dim]
    extended = fetch_rim(paired, axis_dim, 5, False, along_z)
    low_ext = lax.index_in_dim(extended, 0, pair_axis, keepdims=False)
    high_ext = lax.index_in_dim(extended, 1, pair_axis, keepdims=False)
    inner_dim = axis_dim - 1
    if along_z:
        return merge_pair(low_ext, high_ext, inner_dim, coarse_len)
    low_out = rows_product(low_ext, merge_rows(coarse_len, low_taps))
    return low_out + rows_product(high_ext, merge_rows(coarse_len, high_taps))


def spread_mask(keep_part):
    empty_band = jnp.zeros_like(keep_part[:1])
    stacked = jnp.concatenate([empty_band, keep_part], axis=0).astype(jnp.float32)
    z_len = stacked.shape[1]
    y_len = stacked.shape[2]
    x_len = stacked.shape[3]
    grouped = stacked.reshape(2, 2, 2, z_len, y_len, x_len).transpose(0, 1, 3, 4, 2, 5)
    return grouped.reshape(2, 2, z_len, y_len, 2 * x_len)


def on_device(vorticity, keep_one, keep_two, keep_three, keep_four, keep_coarse):
    keep_list = (keep_one, keep_two, keep_three, keep_four)
    x_len = vorticity.shape[-1]
    matrices = [x_matrix(x_len // 2**level_no) for level_no in range(4)]
    approx = vorticity
    kept_list = []
    for level_no in range(4):
        mixed = analyse_axis(approx, 0, 0, True)
        mixed = analyse_axis(mixed, 2, 1, False)
        subbands = x_forward(mixed, matrices[level_no])
        half_len = subbands.shape[-1] // 2
        kept_list.append(subbands * spread_mask(keep_list[level_no]))
        approx = subbands[0, 0, :, :, :half_len]
    rebuilt = approx * keep_coarse.astype(jnp.float32)
    for level_no in (3, 2, 1, 0):
        half_len = rebuilt.shape[-1]
        subbands = kept_list[level_no].at[0, 0, :, :, :half_len].set(rebuilt)
        mixed = x_inverse(subbands, matrices[level_no])
        mixed = join_axis(mixed, 1, 3, False)
        rebuilt = join_axis(mixed, 0, 1, True)
    return rebuilt


def solution(mesh):
    in_specs = (
        P("gz", "gy", None),
        P(None, "gz", "gy", None),
        P(None, "gz", "gy", None),
        P(None, "gz", "gy", None),
        P(None, "gz", "gy", None),
        P("gz", "gy", None),
    )
    out_specs = P("gz", "gy", None)
    return jax.shard_map(
        on_device, mesh=mesh, in_specs=in_specs, out_specs=out_specs, check_vma=False
    )
```

profile of v0, /device:TPU:0, one launch (start us, length us, event | category | flops | bytes accessed | tf_op | source)
XLA Modules:
  0.0 197.2 jit_solution(3459145698990196209)
XLA Ops:
  0.0 2.7 %slice.670 = f32[10,64,512]{2,1,0:T(8,128)} slice(f32[16,64,512]{2,1,0:T(8,128)} %param.14), slice={[0:10], [0:64], [0:512]} | slice | bytes 2621440 | tf_op jit(solution)/shard_map/slice | solution.py:126
  2.7 5.4 %collective-permute-start = (f32[10,64,512]{2,1,0:T(8,128)}, f32[10,64,512]{2,1,0:T(8,128)S(1)}, u32[]{:S(2)}, u32[]{:S(2)}) collective-permute-start(f32[10,64,512]{2,1,0:T(8,128)} %slice.670), channel_id=1, source_target_pairs={{0,30},{2,0},{4,2},{6,4},{8,6},{10,8},{12,10},{14,12},{16,14},{18,... | collective-permute-start | bytes 3932168 | tf_op jit(solution)/shard_map/ppermute | solution.py:25
  28.8 3.0 %copy.64 = f32[2,2,2,8,32,256]{5,2,4,3,1,0:T(2,128)} copy(f32[2,2,2,8,32,256]{5,4,3,2,1,0:T(8,128)S(1)} %bitcast.306) | data formatting | bytes 4194304 | tf_op jit(solution)/shard_map/reshape | solution.py:171
  31.8 4.0 %reshape.3041 = f32[2,2,8,32,512]{4,3,2,1,0:T(8,128)} reshape(f32[2,2,8,32,2,256]{5,4,3,2,1,0:T(2,128)} %bitcast.307) | data formatting | bytes 4194304 | tf_op jit(solution)/shard_map/reshape | solution.py:172
  43.4 8.6 %collective-permute-done.1 = f32[2,8,10,512]{3,2,1,0:T(8,128)S(1)} collective-permute-done((f32[2,8,10,512]{3,2,1,0:T(8,128)S(1)}, f32[2,8,10,512]{3,2,1,0:T(8,128)S(1)}, u32[]{:S(2)}, u32[]{:S(2)}) %collective-permute-start.1) | collective-permute-done | bytes 327712 | tf_op jit(solution)/shard_map/ppermute | solution.py:25
  55.0 5.3 %fusion.1554 = (f32[2,2,8,32,512]{4,3,2,1,0:T(8,128)S(1)}, f32[2,2,8,32,512]{4,3,2,1,0:T(8,128)S(1)}) fusion(f32[2,2,8,32,512]{4,3,2,1,0:T(8,128)S(1)} %copy-done.1, f32[512]{0:T(512)S(1)} %get-tuple-element.82, s32[512]{0:T(512)S(1)} %get-tuple-element.70, f32[512]{0:T(512)S(1)} %get-tuple-element.83, s32[512]{0:T(512)S(1)} %get-tuple-element.71, ...), kind=kOutput, calls=%fused_computation.1756 | convolution fusion | flops 3231449088 | bytes 8437760 | tf_op jit(solution)/shard_map/dot_general | solution.py:108
  60.3 4.1 %collective-permute-start.2 = (f32[8,32,256]{2,1,0:T(8,128)S(1)}, f32[8,32,256]{2,1,0:T(8,128)S(1)}, u32[]{:S(2)}, u32[]{:S(2)}) collective-permute-start(f32[8,32,256]{2,1,0:T(8,128)S(1)} %slice_bitcast_fusion), channel_id=1, source_target_pairs={{0,30},{2,0},{4,2},{6,4},{8,6},{10,8},{12,10},{14,12},{16,14},{18,... | collective-permute-start | bytes 786440 | tf_op jit(solution)/shard_map/ppermute | solution.py:25
  65.4 4.2 %collective-permute-done.3 = f32[2,32,256]{2,1,0:T(8,128)S(1)} collective-permute-done((f32[2,32,256]{2,1,0:T(8,128)S(1)}, f32[2,32,256]{2,1,0:T(8,128)S(1)}, u32[]{:S(2)}, u32[]{:S(2)}) %collective-permute-start.3) | collective-permute-done | bytes 65568 | tf_op jit(solution)/shard_map/ppermute | solution.py:25
  71.7 3.4 %collective-permute-done.4 = f32[2,4,10,256]{3,2,1,0:T(8,128)S(1)} collective-permute-done((f32[2,4,10,256]{3,2,1,0:T(8,128)S(1)}, f32[2,4,10,256]{3,2,1,0:T(8,128)S(1)}, u32[]{:S(2)}, u32[]{:S(2)}) %collective-permute-start.4) | collective-permute-done | bytes 81952 | tf_op jit(solution)/shard_map/ppermute | solution.py:25
  77.2 2.8 %collective-permute-start.5 = (f32[4,16,128]{2,1,0:T(8,128)S(1)}, f32[4,16,128]{2,1,0:T(8,128)S(1)}, u32[]{:S(2)}, u32[]{:S(2)}) collective-permute-start(f32[4,16,128]{2,1,0:T(8,128)S(1)} %slice_bitcast_fusion.2), channel_id=1, source_target_pairs={{0,30},{2,0},{4,2},{6,4},{8,6},{10,8},{12,10},{14,12},{16,14},{18,... | collective-permute-start | bytes 98312 | tf_op jit(solution)/shard_map/ppermute | solution.py:25
  80.0 2.5 %collective-permute-start.6 = (f32[4,16,128]{2,1,0:T(8,128)S(1)}, f32[4,16,128]{2,1,0:T(8,128)S(1)}, u32[]{:S(2)}, u32[]{:S(2)}) collective-permute-start(f32[4,16,128]{2,1,0:T(8,128)S(1)} %slice_bitcast_fusion.2), channel_id=1, source_target_pairs={{0,28},{2,30},{4,0},{6,2},{8,4},{10,6},{12,8},{14,10},{16,12},{18,... | collective-permute-start | bytes 98312 | tf_op jit(solution)/shard_map/ppermute | solution.py:25
  82.5 3.2 %collective-permute-done.7 = f32[2,16,128]{2,1,0:T(8,128)S(1)} collective-permute-done((f32[2,16,128]{2,1,0:T(8,128)S(1)}, f32[2,16,128]{2,1,0:T(8,128)S(1)}, u32[]{:S(2)}, u32[]{:S(2)}) %collective-permute-start.7) | collective-permute-done | bytes 16416 | tf_op jit(solution)/shard_map/ppermute | solution.py:25
  87.5 2.3 %collective-permute-done.8 = f32[2,2,10,128]{3,2,1,0:T(8,128)S(1)} collective-permute-done((f32[2,2,10,128]{3,2,1,0:T(8,128)S(1)}, f32[2,2,10,128]{3,2,1,0:T(8,128)S(1)}, u32[]{:S(2)}, u32[]{:S(2)}) %collective-permute-start.8) | collective-permute-done | bytes 20512 | tf_op jit(solution)/shard_map/ppermute | solution.py:25
  90.7 3.5 %collective-permute-start.10 = (f32[2,8,64]{2,1,0:T(8,128)S(1)}, f32[2,8,64]{2,1,0:T(8,128)S(1)}, u32[]{:S(2)}, u32[]{:S(2)}) collective-permute-start(f32[2,8,64]{2,1,0:T(8,128)S(1)} %slice_bitcast_fusion.8), channel_id=1, source_target_pairs={{0,28},{2,30},{4,0},{6,2},{8,4},{10,6},{12,8},{14,10},{16,12},{18,... | collective-permute-start | bytes 12296 | tf_op jit(solution)/shard_map/ppermute | solution.py:25
  99.6 2.0 %collective-permute-done.14 = f32[2,1,8,64]{3,2,1,0:T(8,128)S(1)} collective-permute-done((f32[2,1,8,64]{3,2,1,0:T(8,128)S(1)}, f32[2,1,8,64]{3,2,1,0:T(8,128)S(1)}, u32[]{:S(2)}, u32[]{:S(2)}) %collective-permute-start.14) | collective-permute-done | bytes 4128 | tf_op jit(solution)/shard_map/ppermute | solution.py:25
  105.9 2.1 %collective-permute-done.17 = f32[2,2,1,4,64]{4,3,1,0,2:T(4,128)S(1)} collective-permute-done((f32[2,2,1,4,64]{4,3,1,0,2:T(4,128)S(1)}, f32[2,2,1,4,64]{4,3,1,0,2:T(4,128)S(1)}, u32[]{:S(2)}, u32[]{:S(2)}) %collective-permute-start.17) | collective-permute-done | bytes 4128 | tf_op jit(solution)/shard_map/ppermute | solution.py:25
  120.0 2.4 %collective-permute-done.23 = f32[2,2,2,5,128]{4,3,2,1,0:T(8,128)S(1)} collective-permute-done((f32[2,2,2,5,128]{4,3,2,1,0:T(8,128)S(1)}, f32[2,2,2,5,128]{4,3,2,1,0:T(8,128)S(1)}, u32[]{:S(2)}, u32[]{:S(2)}) %collective-permute-start.23) | collective-permute-done | bytes 20512 | tf_op jit(solution)/shard_map/ppermute | solution.py:25
  123.0 3.1 %collective-permute-start.25 = (f32[2,2,16,128]{3,2,1,0:T(8,128)S(1)}, f32[2,2,16,128]{3,2,1,0:T(8,128)S(1)}, u32[]{:S(2)}, u32[]{:S(2)}) collective-permute-start(f32[2,2,16,128]{3,2,1,0:T(8,128)S(1)} %fusion.14), channel_id=1, source_target_pairs={{0,4},{2,6},{4,8},{6,10},{8,12},{10,14},{12,16},{14,18},{16,20},{1... | collective-permute-start | bytes 98312 | tf_op jit(solution)/shard_map/ppermute | solution.py:25
  129.6 2.5 %collective-permute-done.24 = f32[2,2,16,128]{3,2,1,0:T(8,128)S(1)} collective-permute-done((f32[2,2,16,128]{3,2,1,0:T(8,128)S(1)}, f32[2,2,16,128]{3,2,1,0:T(8,128)S(1)}, u32[]{:S(2)}, u32[]{:S(2)}) %collective-permute-start.24) | collective-permute-done | bytes 32800 | tf_op jit(solution)/shard_map/ppermute | solution.py:25
  134.6 3.4 %collective-permute-done.27 = f32[2,2,4,5,256]{4,3,2,1,0:T(8,128)S(1)} collective-permute-done((f32[2,2,4,5,256]{4,3,2,1,0:T(8,128)S(1)}, f32[2,2,4,5,256]{4,3,2,1,0:T(8,128)S(1)}, u32[]{:S(2)}, u32[]{:S(2)}) %collective-permute-start.27) | collective-permute-done | bytes 81952 | tf_op jit(solution)/shard_map/ppermute | solution.py:25
  139.4 7.6 %collective-permute-done.29 = f32[2,1,32,256]{3,2,1,0:T(8,128)S(1)} collective-permute-done((f32[2,1,32,256]{3,2,1,0:T(8,128)S(1)}, f32[2,1,32,256]{3,2,1,0:T(8,128)S(1)}, u32[]{:S(2)}, u32[]{:S(2)}) %collective-permute-start.29) | collective-permute-done | bytes 65568 | tf_op jit(solution)/shard_map/ppermute | solution.py:25
  148.5 5.2 %fusion.25 = f32[2,2,8,32,512]{4,3,2,1,0:T(8,128)S(1)} fusion(f32[2,2,8,32,512]{4,3,2,1,0:T(8,128)S(1)} %constant_dynamic-update-slice_fusion.8, f32[512]{0:T(512)S(1)} %get-tuple-element.82, s32[512]{0:T(512)S(1)} %get-tuple-element.70, f32[512]{0:T(512)S(1)} %get-tuple-element.83, s32[512]{0:T(512)S(1)} %get-tuple-element.71, ...), kind=kOutput, calls=%fused_computation.85 | convolution fusion | flops 3230400512 | bytes 4243456 | tf_op jit(solution)/shard_map/dot_general | solution.py:114
  155.4 12.8 %collective-permute-done.30 = f32[2,2,8,5,512]{4,3,2,1,0:T(8,128)S(1)} collective-permute-done((f32[2,2,8,5,512]{4,3,2,1,0:T(8,128)S(1)}, f32[2,2,8,5,512]{4,3,2,1,0:T(8,128)S(1)}, u32[]{:S(2)}, u32[]{:S(2)}) %collective-permute-start.30) | collective-permute-done | bytes 327712 | tf_op jit(solution)/shard_map/ppermute | solution.py:25
  172.3 19.7 %collective-permute-done.31 = f32[2,5,64,512]{3,2,1,0:T(8,128)S(1)} collective-permute-done((f32[2,5,64,512]{3,2,1,0:T(8,128)S(1)}, f32[2,5,64,512]{3,2,1,0:T(8,128)S(1)}, u32[]{:S(2)}, u32[]{:S(2)}) %collective-permute-start.31) | collective-permute-done | bytes 1310752 | tf_op jit(solution)/shard_map/ppermute | solution.py:25
  (318 shorter events, 79.8 us)
Async XLA Ops:
  2.7 37.2 %collective-permute-start = (f32[10,64,512]{2,1,0:T(8,128)}, f32[10,64,512]{2,1,0:T(8,128)S(1)}, u32[]{:S(2)}, u32[]{:S(2)}) collective-permute-start(f32[10,64,512]{2,1,0:T(8,128)} %slice.670), channel_id=1, source_target_pairs={{0,30},{2,0},{4,2},{6,4},{8,6},{10,8},{12,10},{14,12},{16,14},{18,... | collective-permute-start | bytes 3932168 | tf_op jit(solution)/shard_map/ppermute | solution.py:25
  41.8 10.2 %collective-permute-start.1 = (f32[2,8,10,512]{3,2,1,0:T(8,128)S(1)}, f32[2,8,10,512]{3,2,1,0:T(8,128)S(1)}, u32[]{:S(2)}, u32[]{:S(2)}) collective-permute-start(f32[2,8,10,512]{3,2,1,0:T(8,128)S(1)} %pad_maximum_fusion.12), channel_id=1, source_target_pairs={{0,1},{1,0},{2,3},{3,2},{4,5},{5,4},{6,7},{7,6},{8,9},{9,8},{10,11... | collective-permute-start | bytes 983048 | tf_op jit(solution)/shard_map/ppermute | solution.py:25
  60.3 9.4 %collective-permute-start.2 = (f32[8,32,256]{2,1,0:T(8,128)S(1)}, f32[8,32,256]{2,1,0:T(8,128)S(1)}, u32[]{:S(2)}, u32[]{:S(2)}) collective-permute-start(f32[8,32,256]{2,1,0:T(8,128)S(1)} %slice_bitcast_fusion), channel_id=1, source_target_pairs={{0,30},{2,0},{4,2},{6,4},{8,6},{10,8},{12,10},{14,12},{16,14},{18,... | collective-permute-start | bytes 786440 | tf_op jit(solution)/shard_map/ppermute | solution.py:25
  64.4 5.3 %collective-permute-start.3 = (f32[2,32,256]{2,1,0:T(8,128)S(1)}, f32[2,32,256]{2,1,0:T(8,128)S(1)}, u32[]{:S(2)}, u32[]{:S(2)}) collective-permute-start(f32[2,32,256]{2,1,0:T(8,128)S(1)} %slice_bitcast_fusion.1), channel_id=1, source_target_pairs={{0,28},{2,30},{4,0},{6,2},{8,4},{10,6},{12,8},{14,10},{16,12},{18,... | collective-permute-start | bytes 196616 | tf_op jit(solution)/shard_map/ppermute | solution.py:25
  70.1 5.0 %collective-permute-start.4 = (f32[2,4,10,256]{3,2,1,0:T(8,128)S(1)}, f32[2,4,10,256]{3,2,1,0:T(8,128)S(1)}, u32[]{:S(2)}, u32[]{:S(2)}) collective-permute-start(f32[2,4,10,256]{3,2,1,0:T(8,128)S(1)} %pad_maximum_fusion.20), channel_id=1, source_target_pairs={{0,1},{1,0},{2,3},{3,2},{4,5},{5,4},{6,7},{7,6},{8,9},{9,8},{10,11... | collective-permute-start | bytes 245768 | tf_op jit(solution)/shard_map/ppermute | solution.py:25
  77.2 8.5 %collective-permute-start.5 = (f32[4,16,128]{2,1,0:T(8,128)S(1)}, f32[4,16,128]{2,1,0:T(8,128)S(1)}, u32[]{:S(2)}, u32[]{:S(2)}) collective-permute-start(f32[4,16,128]{2,1,0:T(8,128)S(1)} %slice_bitcast_fusion.2), channel_id=1, source_target_pairs={{0,30},{2,0},{4,2},{6,4},{8,6},{10,8},{12,10},{14,12},{16,14},{18,... | collective-permute-start | bytes 98312 | tf_op jit(solution)/shard_map/ppermute | solution.py:25
  80.0 5.7 %collective-permute-start.6 = (f32[4,16,128]{2,1,0:T(8,128)S(1)}, f32[4,16,128]{2,1,0:T(8,128)S(1)}, u32[]{:S(2)}, u32[]{:S(2)}) collective-permute-start(f32[4,16,128]{2,1,0:T(8,128)S(1)} %slice_bitcast_fusion.2), channel_id=1, source_target_pairs={{0,28},{2,30},{4,0},{6,2},{8,4},{10,6},{12,8},{14,10},{16,12},{18,... | collective-permute-start | bytes 98312 | tf_op jit(solution)/shard_map/ppermute | solution.py:25
  85.7 4.0 %collective-permute-start.8 = (f32[2,2,10,128]{3,2,1,0:T(8,128)S(1)}, f32[2,2,10,128]{3,2,1,0:T(8,128)S(1)}, u32[]{:S(2)}, u32[]{:S(2)}) collective-permute-start(f32[2,2,10,128]{3,2,1,0:T(8,128)S(1)} %pad_maximum_fusion.26), channel_id=1, source_target_pairs={{0,1},{1,0},{2,3},{3,2},{4,5},{5,4},{6,7},{7,6},{8,9},{9,8},{10,11... | collective-permute-start | bytes 61448 | tf_op jit(solution)/shard_map/ppermute | solution.py:25
  90.7 4.9 %collective-permute-start.10 = (f32[2,8,64]{2,1,0:T(8,128)S(1)}, f32[2,8,64]{2,1,0:T(8,128)S(1)}, u32[]{:S(2)}, u32[]{:S(2)}) collective-permute-start(f32[2,8,64]{2,1,0:T(8,128)S(1)} %slice_bitcast_fusion.8), channel_id=1, source_target_pairs={{0,28},{2,30},{4,0},{6,2},{8,4},{10,6},{12,8},{14,10},{16,12},{18,... | collective-permute-start | bytes 12296 | tf_op jit(solution)/shard_map/ppermute | solution.py:25
  97.9 3.7 %collective-permute-start.14 = (f32[2,1,8,64]{3,2,1,0:T(8,128)S(1)}, f32[2,1,8,64]{3,2,1,0:T(8,128)S(1)}, u32[]{:S(2)}, u32[]{:S(2)}) collective-permute-start(f32[2,1,8,64]{3,2,1,0:T(8,128)S(1)} %pad_maximum_fusion.32), channel_id=1, source_target_pairs={{0,1},{1,0},{2,3},{3,2},{4,5},{5,4},{6,7},{7,6},{8,9},{9,8},{10,11... | collective-permute-start | bytes 12296 | tf_op jit(solution)/shard_map/ppermute | solution.py:25
  108.5 5.8 %collective-permute-start.18 = (f32[2,1,8,64]{3,2,1,0:T(8,128)S(1)}, f32[2,1,8,64]{3,2,1,0:T(8,128)S(1)}, u32[]{:S(2)}, u32[]{:S(2)}) collective-permute-start(f32[2,1,8,64]{3,2,1,0:T(8,128)S(1)} %fusion.15), channel_id=1, source_target_pairs={{0,2},{2,4},{4,6},{6,8},{8,10},{10,12},{12,14},{14,16},{16,18},{18... | collective-permute-start | bytes 12296 | tf_op jit(solution)/shard_map/ppermute | solution.py:25
  108.5 6.4 %collective-permute-start.19 = (f32[2,1,8,64]{3,2,1,0:T(8,128)S(1)}, f32[2,1,8,64]{3,2,1,0:T(8,128)S(1)}, u32[]{:S(2)}, u32[]{:S(2)}) collective-permute-start(f32[2,1,8,64]{3,2,1,0:T(8,128)S(1)} %fusion.15), channel_id=1, source_target_pairs={{0,4},{2,6},{4,8},{6,10},{8,12},{10,14},{12,16},{14,18},{16,20},{1... | collective-permute-start | bytes 12296 | tf_op jit(solution)/shard_map/ppermute | solution.py:25
  109.9 5.0 %collective-permute-start.20 = (f32[2,1,8,64]{3,2,1,0:T(8,128)S(1)}, f32[2,1,8,64]{3,2,1,0:T(8,128)S(1)}, u32[]{:S(2)}, u32[]{:S(2)}) collective-permute-start(f32[2,1,8,64]{3,2,1,0:T(8,128)S(1)} %fusion.15), channel_id=1, source_target_pairs={{0,6},{2,8},{4,10},{6,12},{8,14},{10,16},{12,18},{14,20},{16,22},{... | collective-permute-start | bytes 12296 | tf_op jit(solution)/shard_map/ppermute | solution.py:25
  111.1 5.4 %collective-permute-start.21 = (f32[2,1,8,64]{3,2,1,0:T(8,128)S(1)}, f32[2,1,8,64]{3,2,1,0:T(8,128)S(1)}, u32[]{:S(2)}, u32[]{:S(2)}) collective-permute-start(f32[2,1,8,64]{3,2,1,0:T(8,128)S(1)} %fusion.15), channel_id=1, source_target_pairs={{0,8},{2,10},{4,12},{6,14},{8,16},{10,18},{12,20},{14,22},{16,24},... | collective-permute-start | bytes 12296 | tf_op jit(solution)/shard_map/ppermute | solution.py:25
  112.9 4.9 %collective-permute-start.22 = (f32[2,1,8,64]{3,2,1,0:T(8,128)S(1)}, f32[2,1,8,64]{3,2,1,0:T(8,128)S(1)}, u32[]{:S(2)}, u32[]{:S(2)}) collective-permute-start(f32[2,1,8,64]{3,2,1,0:T(8,128)S(1)} %fusion.15), channel_id=1, source_target_pairs={{0,10},{2,12},{4,14},{6,16},{8,18},{10,20},{12,22},{14,24},{16,26}... | collective-permute-start | bytes 12296 | tf_op jit(solution)/shard_map/ppermute | solution.py:25
  118.4 4.0 %collective-permute-start.23 = (f32[2,2,2,5,128]{4,3,2,1,0:T(8,128)S(1)}, f32[2,2,2,5,128]{4,3,2,1,0:T(8,128)S(1)}, u32[]{:S(2)}, u32[]{:S(2)}) collective-permute-start(f32[2,2,2,5,128]{4,3,2,1,0:T(8,128)S(1)} %slice.827), channel_id=1, source_target_pairs={{0,1},{1,0},{2,3},{3,2},{4,5},{5,4},{6,7},{7,6},{8,9},{9,8},{10,11... | collective-permute-start | bytes 61448 | tf_op jit(solution)/shard_map/ppermute | solution.py:25
  122.9 5.0 %collective-permute-start.26 = (f32[2,1,16,128]{3,2,1,0:T(8,128)S(1)}, f32[2,1,16,128]{3,2,1,0:T(8,128)S(1)}, u32[]{:S(2)}, u32[]{:S(2)}) collective-permute-start(f32[2,1,16,128]{3,2,1,0:T(8,128)S(1)} %slice.838), channel_id=1, source_target_pairs={{0,6},{2,8},{4,10},{6,12},{8,14},{10,16},{12,18},{14,20},{16,22},{... | collective-permute-start | bytes 49160 | tf_op jit(solution)/shard_map/ppermute | solution.py:25
  123.0 6.7 %collective-permute-start.25 = (f32[2,2,16,128]{3,2,1,0:T(8,128)S(1)}, f32[2,2,16,128]{3,2,1,0:T(8,128)S(1)}, u32[]{:S(2)}, u32[]{:S(2)}) collective-permute-start(f32[2,2,16,128]{3,2,1,0:T(8,128)S(1)} %fusion.14), channel_id=1, source_target_pairs={{0,4},{2,6},{4,8},{6,10},{8,12},{10,14},{12,16},{14,18},{16,20},{1... | collective-permute-start | bytes 98312 | tf_op jit(solution)/shard_map/ppermute | solution.py:25
  126.1 6.0 %collective-permute-start.24 = (f32[2,2,16,128]{3,2,1,0:T(8,128)S(1)}, f32[2,2,16,128]{3,2,1,0:T(8,128)S(1)}, u32[]{:S(2)}, u32[]{:S(2)}) collective-permute-start(f32[2,2,16,128]{3,2,1,0:T(8,128)S(1)} %fusion.14), channel_id=1, source_target_pairs={{0,2},{2,4},{4,6},{6,8},{8,10},{10,12},{12,14},{14,16},{16,18},{18... | collective-permute-start | bytes 98312 | tf_op jit(solution)/shard_map/ppermute | solution.py:25
  133.0 5.0 %collective-permute-start.27 = (f32[2,2,4,5,256]{4,3,2,1,0:T(8,128)S(1)}, f32[2,2,4,5,256]{4,3,2,1,0:T(8,128)S(1)}, u32[]{:S(2)}, u32[]{:S(2)}) collective-permute-start(f32[2,2,4,5,256]{4,3,2,1,0:T(8,128)S(1)} %slice.841), channel_id=1, source_target_pairs={{0,1},{1,0},{2,3},{3,2},{4,5},{5,4},{6,7},{7,6},{8,9},{9,8},{10,11... | collective-permute-start | bytes 245768 | tf_op jit(solution)/shard_map/ppermute | solution.py:25
  138.9 9.2 %collective-permute-start.28 = (f32[2,4,32,256]{3,2,1,0:T(8,128)S(1)}, f32[2,4,32,256]{3,2,1,0:T(8,128)S(1)}, u32[]{:S(2)}, u32[]{:S(2)}) collective-permute-start(f32[2,4,32,256]{3,2,1,0:T(8,128)S(1)} %fusion.13), channel_id=1, source_target_pairs={{0,2},{2,4},{4,6},{6,8},{8,10},{10,12},{12,14},{14,16},{16,18},{18... | collective-permute-start | bytes 786440 | tf_op jit(solution)/shard_map/ppermute | solution.py:25
  139.0 8.0 %collective-permute-start.29 = (f32[2,1,32,256]{3,2,1,0:T(8,128)S(1)}, f32[2,1,32,256]{3,2,1,0:T(8,128)S(1)}, u32[]{:S(2)}, u32[]{:S(2)}) collective-permute-start(f32[2,1,32,256]{3,2,1,0:T(8,128)S(1)} %slice.858), channel_id=1, source_target_pairs={{0,4},{2,6},{4,8},{6,10},{8,12},{10,14},{12,16},{14,18},{16,20},{1... | collective-permute-start | bytes 196616 | tf_op jit(solution)/shard_map/ppermute | solution.py:25
  153.8 14.4 %collective-permute-start.30 = (f32[2,2,8,5,512]{4,3,2,1,0:T(8,128)S(1)}, f32[2,2,8,5,512]{4,3,2,1,0:T(8,128)S(1)}, u32[]{:S(2)}, u32[]{:S(2)}) collective-permute-start(f32[2,2,8,5,512]{4,3,2,1,0:T(8,128)S(1)} %slice.861), channel_id=1, source_target_pairs={{0,1},{1,0},{2,3},{3,2},{4,5},{5,4},{6,7},{7,6},{8,9},{9,8},{10,11... | collective-permute-start | bytes 983048 | tf_op jit(solution)/shard_map/ppermute | solution.py:25
  172.2 19.8 %collective-permute-start.31 = (f32[2,5,64,512]{3,2,1,0:T(8,128)S(1)}, f32[2,5,64,512]{3,2,1,0:T(8,128)S(1)}, u32[]{:S(2)}, u32[]{:S(2)}) collective-permute-start(f32[2,5,64,512]{3,2,1,0:T(8,128)S(1)} %slice.866), channel_id=1, source_target_pairs={{0,2},{2,4},{4,6},{6,8},{8,10},{10,12},{12,14},{14,16},{16,18},{18... | collective-permute-start | bytes 3932168 | tf_op jit(solution)/shard_map/ppermute | solution.py:25
  (67 other events, 953.9 us)
where the time goes:
time: 197 us
  waiting for transfers between devices  86.1 us (44%)
  starting transfers between devices  41.5 us (21%)
  other arithmetic  26.8 us (14%)
  matrix products  24.6 us (12%)
  local copies, waits for them, and re-layouts  16.7 us (8%)
    ppermute x32, waiting for transfers between devices, shifted(): lax.ppermute(shard, axis, [(i, (i + by) % devices) for i in range(devices)])  86.1 us
    ppermute x32, starting transfers between devices, shifted(): lax.ppermute(shard, axis, [(i, (i + by) % devices) for i in range(devices)])  41.5 us
    dot_general x16, matrix products, rows_product(): jnp.einsum('...yx,ky->...kx', source, matrix, precision=lax.Precision.HIG...  10.1 us
    select_n x24, other arithmetic, x_matrix(): is_hit = (2 * col_pos + k) % x_len == row_ids  8.81 us
    select_n x24, other arithmetic, x_matrix(): jnp.where(is_low, low_taps[k], high_taps[k])  8.66 us
    dot_general x4, matrix products, x_forward(): jnp.dot(source, matrix, precision=lax.Precision.HIGHEST, preferred_elemen...  7.27 us
    dot_general x4, matrix products, x_inverse(): jnp.dot(source, matrix.T, precision=lax.Precision.HIGHEST, preferred_elem...  7.21 us
    reshape x4, local copies, waits for them, and re-layouts, spread_mask(): return grouped.reshape(2, 2, z_len, y_len, 2 * x_len)  6.11 us
  transfers between devices with their start and end apart: 32, of which 23 were waited for; matrix products, arithmetic and copies ran while one was open for 16% of the time, Pallas kernels for 0%

commit v1 on v0

v1 whole, which is shorter than its diff:
```python
import functools

import jax
import jax.numpy as jnp
import ml_dtypes
import numpy as np
from jax import lax
from jax.experimental import pallas as pl
from jax.experimental.pallas import tpu as pltpu
from jax.sharding import PartitionSpec as P

low_taps = (
    0.11154074335008017,
    0.4946238903983854,
    0.7511339080215775,
    0.3152503517092432,
    -0.22626469396516913,
    -0.12976686756709563,
    0.09750160558707936,
    0.02752286553001629,
    -0.031582039318031156,
    0.0005538422009938016,
    0.004777257511010651,
    -0.00107730108499558,
)
high_taps = tuple(((-1.0) ** k * low_taps[11 - k] for k in range(12)))
LEVELS = 4
MESH = pl.DeviceIdType.MESH
BF16 = jnp.bfloat16
F32 = jnp.float32


def halves(matrix):
    matrix = matrix.astype(np.float32)
    high = matrix.astype(ml_dtypes.bfloat16)
    low = (matrix - high.astype(np.float32)).astype(ml_dtypes.bfloat16)
    return np.stack([high, low])


def x_matrix(x_len):
    half = x_len // 2
    matrix = np.zeros((x_len, x_len))
    for i in range(half):
        for k in range(12):
            matrix[(2 * i + k) % x_len, i] += low_taps[k]
            matrix[(2 * i + k) % x_len, half + i] += high_taps[k]
    return matrix


def y_split_matrix(y_len, ext_len):
    half = y_len // 2
    matrix = np.zeros((y_len, ext_len))
    for i in range(half):
        for k in range(12):
            matrix[i, 2 * i + k] = low_taps[k]
            matrix[half + i, 2 * i + k] = high_taps[k]
    return matrix


def y_merge_matrix(coarse, ext_len):
    first = ext_len - coarse
    matrix = np.zeros((2 * coarse, 2 * ext_len))
    for j in range(2 * coarse):
        for t in range(6):
            k = 2 * t + j % 2
            c = j // 2 - t + first
            matrix[j, c] = low_taps[k]
            matrix[j, ext_len + c] = high_taps[k]
    return matrix


class Level:
    def __init__(self, z, y, x):
        self.z, self.y, self.x = z, y, x
        self.zc, self.yc, self.xc = z // 2, y // 2, x // 2
        self.rim_rows = min(y, 16)
        self.rim_hops = 16 // self.rim_rows
        self.y_ext = y + 16
        self.z_ext = z + 10
        self.block = min(self.yc, 8)
        self.back_hops = 8 // self.block
        self.blocks = self.yc // self.block + self.back_hops
        self.yc_ext = self.blocks * self.block
        self.zc_ext = self.zc + 5


def hop_list(length, rim):
    pieces = [(0, 0, length)]
    done = 0
    hop = 1
    while done < rim:
        take = min(length, rim - done)
        pieces.append((hop, done, take))
        done += take
        hop += 1
    return pieces


def split_product(data, pair_ref):
    high = data.astype(BF16)
    low = (data - high.astype(F32)).astype(BF16)
    out = jnp.dot(high, pair_ref[0], preferred_element_type=F32)
    out += jnp.dot(low, pair_ref[0], preferred_element_type=F32)
    return out + jnp.dot(high, pair_ref[1], preferred_element_type=F32)


def product_split(pair_ref, data):
    high = data.astype(BF16)
    low = (data - high.astype(F32)).astype(BF16)
    out = jnp.dot(pair_ref[0], high, preferred_element_type=F32)
    out += jnp.dot(pair_ref[0], low, preferred_element_type=F32)
    return out + jnp.dot(pair_ref[1], high, preferred_element_type=F32)


def kernel(levels, nz, ny, count, *refs):
    field = refs[0]
    keeps = refs[1:5]
    coarse = refs[5]
    x_fwd = refs[6:10]
    x_inv = refs[10:14]
    y_fwd = refs[14:18]
    y_inv = refs[18:22]
    out = refs[22]
    exts = refs[23:27]
    zbufs = refs[27:31]
    coefs = refs[31:35]
    sbufs = refs[35:39]
    ybufs = refs[39:43]
    local_sem, send_sem, recv_sem = refs[43:46]
    gz = lax.axis_index("gz")
    gy = lax.axis_index("gy")

    def device(dz, dy):
        return (lax.rem(gz + (dz + nz) % nz, nz), lax.rem(gy + (dy + ny) % ny, ny))

    load = pltpu.make_async_copy(field, exts[0].at[0 : levels[0].z, 0 : levels[0].y], local_sem)
    load.start()
    offsets = sorted(
        {(dz % nz, dy % ny) for dz in range(-5, 6) for dy in range(-2, 3)} - {(0, 0)}
    )
    barrier = pltpu.get_barrier_semaphore()
    for dz, dy in offsets:
        pl.semaphore_signal(barrier, inc=1, device_id=device(dz, dy), device_id_type=MESH)
    pl.semaphore_wait(barrier, len(offsets))

    used = [0]
    sends = []

    def send(src, dst, dz, dy):
        at = used[0]
        used[0] += 1
        copy = pltpu.make_async_remote_copy(
            src_ref=src,
            dst_ref=dst,
            send_sem=send_sem.at[at],
            recv_sem=recv_sem.at[at],
            device_id=device(dz, dy),
            device_id_type=MESH,
        )
        copy.start()
        sends.append(copy)
        return copy

    def send_rim(lv, source, ext):
        copies = []
        for hz, z_at, z_take in hop_list(lv.z, 10):
            for hy in range(lv.rim_hops + 1):
                if hy and hy % ny == 0 or (hz == 0 and hy == 0):
                    continue
                rows = lv.y if hy == 0 else lv.rim_rows
                z_to = 0 if hz == 0 else lv.z + z_at
                y_to = 0 if hy == 0 else lv.y + (hy - 1) * lv.rim_rows
                copies.append(
                    send(
                        source.at[0:z_take, 0:rows],
                        ext.at[z_to : z_to + z_take, y_to : y_to + rows],
                        -hz,
                        -hy,
                    )
                )
        return copies

    def send_back(lv, coef, first, last):
        copies = []
        own = lv.back_hops
        for hz, z_at, z_take in hop_list(lv.zc, 5):
            for hy in range(lv.back_hops + 1):
                if hy and hy % ny == 0 or (hz == 0 and hy == 0):
                    continue
                z_from = 5 if hz == 0 else 5 + lv.zc - z_take
                z_to = 5 if hz == 0 else 5 - z_at - z_take
                y_from = own if hy == 0 else lv.blocks - 1
                y_take = lv.blocks - own if hy == 0 else 1
                y_to = own if hy == 0 else own - hy
                copies.append(
                    send(
                        coef.at[first:last, z_from : z_from + z_take, y_from : y_from + y_take],
                        coef.at[first:last, z_to : z_to + z_take, y_to : y_to + y_take],
                        hz,
                        hy,
                    )
                )
        return copies

    detail_copies = []
    for no, lv in enumerate(levels):
        ext, zbuf, coef, keep = exts[no], zbufs[no], coefs[no], keeps[no]
        copies = send_rim(lv, field if no == 0 else ext, ext)
        if no == 0:
            load.wait()
        for copy in copies:
            copy.wait_recv()
        for hy in range(1, lv.rim_hops + 1):
            if hy % ny == 0:
                y_to = lv.y + (hy - 1) * lv.rim_rows
                ext[:, y_to : y_to + lv.rim_rows, :] = ext[:, 0 : lv.rim_rows, :]
        chunk = 16 if lv.y_ext % 16 == 0 else 8
        steps = lv.y_ext // chunk

        def z_split(step, carry, lv=lv, ext=ext, zbuf=zbuf, chunk=chunk, steps=steps):
            i = step // steps
            row = pl.multiple_of((step % steps) * chunk, chunk)
            low = high = None
            for k in range(12):
                part = ext[2 * i + k, pl.ds(row, chunk), :]
                low = low_taps[k] * part if k == 0 else low + low_taps[k] * part
                high = high_taps[k] * part if k == 0 else high + high_taps[k] * part
            zbuf[i, pl.ds(row, chunk), :] = low
            zbuf[lv.zc + i, pl.ds(row, chunk), :] = high
            return carry

        lax.fori_loop(0, lv.zc * steps, z_split, 0)
        group = min(lv.z, 4)

        def x_split(step, carry, lv=lv, zbuf=zbuf, group=group, no=no):
            at = pl.ds(step * group, group)
            rows = zbuf[at].reshape(group * lv.y_ext, lv.x)
            zbuf[at] = split_product(rows, x_fwd[no]).reshape(group, lv.y_ext, lv.x)
            return carry

        lax.fori_loop(0, lv.z // group, x_split, 0)

        def y_split(i, carry, lv=lv, zbuf=zbuf, coef=coef, keep=keep, no=no):
            for bz in range(2):
                mixed = product_split(y_fwd[no], zbuf[bz * lv.zc + i])
                for by in range(2):
                    part = mixed[by * lv.yc : (by + 1) * lv.yc]
                    for bx in range(2):
                        band = 4 * bz + 2 * by + bx
                        piece = part[:, bx * lv.xc : (bx + 1) * lv.xc]
                        if band:
                            piece = piece * keep[band - 1, i].astype(F32)
                        elif no < LEVELS - 1:
                            exts[no + 1][i, 0 : lv.yc, :] = piece
                            continue
                        else:
                            piece = piece * coarse[i].astype(F32)
                        shaped = piece.reshape(lv.yc // lv.block, lv.block, lv.xc)
                        lanes = slice(bx * lv.xc, (bx + 1) * lv.xc)
                        coef[2 * bz + by, 5 + i, lv.back_hops : lv.blocks, :, lanes] = shaped
            return carry

        lax.fori_loop(0, lv.zc, y_split, 0)
        if no == LEVELS - 1:
            detail_copies.append([])
        else:
            detail_copies.append((lv, coef))

    early = [None] * LEVELS
    for no in range(LEVELS - 1, -1, -1):
        lv, coef, sbuf, ybuf = levels[no], coefs[no], sbufs[no], ybufs[no]
        late = send_back(lv, coef, 0, 1)
        if no == LEVELS - 1:
            for each in range(LEVELS - 1, -1, -1):
                early[each] = send_back(levels[each], coefs[each], 1, 4)
        for copy in late + early[no]:
            copy.wait_recv()
        for hy in range(1, lv.back_hops + 1):
            if hy % ny == 0:
                coef[:, :, lv.back_hops - hy] = coef[:, :, lv.blocks - 1]
        z_group = lv.zc_ext

        def x_merge(b, carry, lv=lv, coef=coef, sbuf=sbuf, no=no):
            if lv.block == 8:
                rows = coef[b].reshape(lv.zc_ext * lv.yc_ext, lv.x)
                sbuf[b] = split_product(rows, x_inv[no]).reshape(lv.zc_ext, lv.yc_ext, lv.x)
            else:
                for z in range(lv.zc_ext):
                    rows = jnp.concatenate([coef[b, z, j] for j in range(lv.blocks)], axis=0)
                    sbuf[b, z] = split_product(rows, x_inv[no])
            return carry

        lax.fori_loop(0, 4, x_merge, 0)

        def y_merge(z, carry, lv=lv, sbuf=sbuf, ybuf=ybuf, no=no):
            for bz in range(2):
                pair = jnp.concatenate([sbuf[2 * bz, z], sbuf[2 * bz + 1, z]], axis=0)
                ybuf[bz, z] = product_split(y_inv[no], pair)
            return carry

        lax.fori_loop(0, lv.zc_ext, y_merge, 0)
        chunk = min(lv.y, 16)
        if no:
            chunk = min(chunk, levels[no - 1].block)
        steps = lv.y // chunk

        def z_merge(step, carry, lv=lv, ybuf=ybuf, no=no, chunk=chunk, steps=steps):
            i = step // steps
            at = step % steps
            row = pl.multiple_of(at * chunk, chunk)
            even = odd = None
            for t in range(6):
                low = ybuf[0, i + 5 - t, pl.ds(row, chunk), :]
                high = ybuf[1, i + 5 - t, pl.ds(row, chunk), :]
                even_term = low_taps[2 * t] * low + high_taps[2 * t] * high
                odd_term = low_taps[2 * t + 1] * low + high_taps[2 * t + 1] * high
                even = even_term if t == 0 else even + even_term
                odd = odd_term if t == 0 else odd + odd_term
            for p, value in ((0, even), (1, odd)):
                if no == 0:
                    out[2 * i + p, pl.ds(row, chunk), :] = value
                else:
                    own = levels[no - 1].back_hops
                    coefs[no - 1][0, 5 + 2 * i + p, own + at, :, 0 : lv.x] = value
            return carry

        lax.fori_loop(0, lv.zc * steps, z_merge, 0)
    for copy in sends:
        copy.wait_send()
    assert used[0] == count


def solution(mesh):
    nz, ny = mesh.shape["gz"], mesh.shape["gy"]

    def on_device(field, k1, k2, k3, k4, coarse):
        z, y, x = field.shape
        levels = [Level(z >> n, y >> n, x >> n) for n in range(LEVELS)]
        count = 0
        for lv in levels:
            rim = len(hop_list(lv.z, 10)) * sum(h % ny != 0 or h == 0 for h in range(lv.rim_hops + 1))
            back = len(hop_list(lv.zc, 5)) * sum(h % ny != 0 or h == 0 for h in range(lv.back_hops + 1))
            count += rim - 1 + 2 * (back - 1)
        x_pairs = [halves(x_matrix(lv.x)) for lv in levels]
        xt_pairs = [halves(x_matrix(lv.x).T) for lv in levels]
        y_pairs = [halves(y_split_matrix(lv.y, lv.y_ext)) for lv in levels]
        yt_pairs = [halves(y_merge_matrix(lv.yc, lv.yc_ext)) for lv in levels]
        mats = [jnp.asarray(m) for m in x_pairs + xt_pairs + y_pairs + yt_pairs]
        vmem = pl.BlockSpec(memory_space=pltpu.VMEM)
        scratch = [pltpu.VMEM((lv.z_ext, lv.y_ext, lv.x), F32) for lv in levels]
        scratch += [pltpu.VMEM((lv.z, lv.y_ext, lv.x), F32) for lv in levels]
        scratch += [pltpu.VMEM((4, lv.zc_ext, lv.blocks, lv.block, lv.x), F32) for lv in levels]
        scratch += [pltpu.VMEM((4, lv.zc_ext, lv.yc_ext, lv.x), F32) for lv in levels]
        scratch += [pltpu.VMEM((2, lv.zc_ext, lv.y, lv.x), F32) for lv in levels]
        scratch += [
            pltpu.SemaphoreType.DMA,
            pltpu.SemaphoreType.DMA((count,)),
            pltpu.SemaphoreType.DMA((count,)),
        ]
        return pl.pallas_call(
            functools.partial(kernel, levels, nz, ny, count),
            out_shape=jax.ShapeDtypeStruct((z, y, x), F32),
            in_specs=[pl.BlockSpec(memory_space=pl.ANY)] + [vmem] * (5 + len(mats)),
            out_specs=vmem,
            scratch_shapes=scratch,
            compiler_params=pltpu.CompilerParams(
                collective_id=0, has_side_effects=True, vmem_limit_bytes=60 * 1024 * 1024
            ),
        )(field, k1, k2, k3, k4, coarse, *mats)

    in_specs = (
        P("gz", "gy", None),
        P(None, "gz", "gy", None),
        P(None, "gz", "gy", None),
        P(None, "gz", "gy", None),
        P(None, "gz", "gy", None),
        P("gz", "gy", None),
    )
    return jax.shard_map(
        on_device, mesh=mesh, in_specs=in_specs, out_specs=P("gz", "gy", None), check_vma=False
    )
```

time: 197 us -> 116 us (0.59)
  Pallas kernels: 0 us -> 112 us
  waiting for transfers between devices: 86.1 us -> 0 us
  starting transfers between devices: 41.5 us -> 0 us
  other arithmetic: 26.8 us -> 0 us
  matrix products: 24.6 us -> 0 us
  local copies, waits for them, and re-layouts: 16.7 us -> 3.14 us
    pallas_call x0 -> x1, Pallas kernels: none -> 112 us  [on_device(): pl.pallas_call(functools.partial(kernel, levels, nz, ny, count), out_shap...]
    ppermute x32 -> x0, waiting for transfers between devices: 86.1 us -> none  [shifted(): lax.ppermute(shard, axis, [(i, (i + by) % devices) for i in range(devices)])]
    ppermute x32 -> x0, starting transfers between devices: 41.5 us -> none  [shifted(): lax.ppermute(shard, axis, [(i, (i + by) % devices) for i in range(devices)])]
    dot_general x24 -> x0, matrix products: 24.6 us -> none  [the longest x16 10.1 us: rows_product(): jnp.einsum('...yx,ky->...kx', source, matrix, precision=lax.Precision.HIG...]
    select_n x52 -> x0, other arithmetic: 18.1 us -> none  [the longest x24 8.81 us: x_matrix(): is_hit = (2 * col_pos + k) % x_len == row_ids]
    reshape x8 -> x0, local copies, waits for them, and re-layouts: 11 us -> none  [the longest x4 6.11 us: spread_mask(): return grouped.reshape(2, 2, z_len, y_len, 2 * x_len)]
    add x9 -> x0, other arithmetic: 3.62 us -> none  [the longest x4 1.81 us: merge_pair(): even_part = even_part + even_term]
    slice x10 -> x0, local copies, waits for them, and re-layouts: 2.9 us -> none  [the longest x3 2.66 us: fetch_rim(): sliced = lax.slice_in_dim(source, 0, take_len, axis=axis_dim)]
  transfers between devices with their start and end apart: 32 -> 0, of which waited for: 23 -> 0; matrix products, arithmetic and copies ran while one was open for 16% -> 0% of each run, Pallas kernels for 0% -> 0%
where the time goes in v1:
time: 116 us; the launch traced here: 115 us
  Pallas kernels  112 us (97%)
  local copies, waits for them, and re-layouts  3.14 us (3%)
    pallas_call x1, Pallas kernels, on_device(): pl.pallas_call(functools.partial(kernel, levels, nz, ny, count), out_shap...  112 us
    unnamed x1, local copies, waits for them, and re-layouts  3.14 us

profile of v1, /device:TPU:0, one launch (start us, length us, event | category | flops | bytes accessed | tf_op | source)
XLA Modules:
  0.0 115.0 jit_solution(16442185779330798715)
XLA Ops:
  0.0 111.8 %shard_map.208 = f32[16,64,512]{2,1,0:T(8,128)} custom-call(f32[16,64,512]{2,1,0:T(8,128)} %refs_0_.1, s32[7,8,32,256]{3,2,1,0:T(8,128)} %refs_1_.1, s32[7,4,16,128]{3,2,1,0:T(8,128)} %refs_2_.1, s32[7,2,8,64]{3,2,1,0:T(8,128)} %refs_3_.1, s32[7,1,4,32]{3,2,1,0:T(4,128)} %refs_4_.1, s32[1,4,32]{2,1,0:T(4,128)} %refs_5_.1, ...), custom_call_target="tpu_custom_call" | custom-call | tf_op jit(solution)/shard_map/pallas_call | solution.py:360
  111.8 3.1 %copy.24 = f32[16,64,512]{2,1,0:T(8,128)} copy(f32[16,64,512]{2,1,0:T(8,128)} %shard_map.208) | data formatting | bytes 4194304

commit v2 on v1

--- a/solution.py
+++ b/solution.py
@@ -121,19 +121,20 @@
     y_fwd = refs[14:18]
     y_inv = refs[18:22]
     out = refs[22]
-    exts = refs[23:27]
-    zbufs = refs[27:31]
-    coefs = refs[31:35]
-    sbufs = refs[35:39]
-    ybufs = refs[39:43]
-    local_sem, send_sem, recv_sem = refs[43:46]
+    whole, mixed_x, mixed_y = refs[23:26]
+    exts = (None,) + refs[26:29]
+    zbufs = (None,) + refs[29:32]
+    coefs = refs[32:36]
+    sbufs = refs[36:40]
+    ybufs = refs[40:44]
+    local_sem, send_sem, recv_sem = refs[44:47]
     gz = lax.axis_index("gz")
     gy = lax.axis_index("gy")
 
     def device(dz, dy):
         return (lax.rem(gz + (dz + nz) % nz, nz), lax.rem(gy + (dy + ny) % ny, ny))
 
-    load = pltpu.make_async_copy(field, exts[0].at[0 : levels[0].z, 0 : levels[0].y], local_sem)
+    load = pltpu.make_async_copy(field, whole, local_sem)
     load.start()
     offsets = sorted(
         {(dz % nz, dy % ny) for dz in range(-5, 6) for dy in range(-2, 3)} - {(0, 0)}
@@ -141,7 +142,6 @@
     barrier = pltpu.get_barrier_semaphore()
     for dz, dy in offsets:
         pl.semaphore_signal(barrier, inc=1, device_id=device(dz, dy), device_id_type=MESH)
-    pl.semaphore_wait(barrier, len(offsets))
 
     used = [0]
     sends = []
@@ -180,7 +180,7 @@
                 )
         return copies
 
-    def send_back(lv, coef, first, last):
+    def send_back(lv, coef, first, last, lanes=slice(None)):
         copies = []
         own = lv.back_hops
         for hz, z_at, z_take in hop_list(lv.zc, 5):
@@ -194,20 +194,108 @@
                 y_to = own if hy == 0 else own - hy
                 copies.append(
                     send(
-                        coef.at[first:last, z_from : z_from + z_take, y_from : y_from + y_take],
-                        coef.at[first:last, z_to : z_to + z_take, y_to : y_to + y_take],
+                        coef.at[first:last, z_from : z_from + z_take, y_from : y_from + y_take, :, lanes],
+                        coef.at[first:last, z_to : z_to + z_take, y_to : y_to + y_take, :, lanes],
                         hz,
                         hy,
                     )
                 )
         return copies
 
-    detail_copies = []
+    first = levels[0]
+    half = first.xc
+    rim = first.rim_rows
+    assert first.rim_hops == 1 and first.z >= 10 and first.back_hops == 1
+
+    load.wait()
+    rows = whole[:, 0:rim, :].reshape(first.z * rim, first.x)
+    mixed_x[:, 0:rim, :] = split_product(rows, x_fwd[0]).reshape(first.z, rim, first.x)
+    pl.semaphore_wait(barrier, len(offsets))
+    y_low, y_high = [
+        send(
+            mixed_x.at[:, 0:rim, lanes],
+            mixed_x.at[:, first.y : first.y + rim, lanes],
+            0,
+            -1,
+        )
+        for lanes in (slice(0, half), slice(half, first.x))
+    ]
+
+    def x_rest(step, carry):
+        at = pl.ds(step * 4, 4)
+        rest = whole[at, rim : first.y, :].reshape(4 * (first.y - rim), first.x)
+        done = split_product(rest, x_fwd[0])
+        mixed_x[at, rim : first.y, :] = done.reshape(4, first.y - rim, first.x)
+        return carry
+
+    lax.fori_loop(0, first.z // 4, x_rest, 0)
+
+    def y_planes(start, stop, lanes):
+        def y_plane(z, carry):
+            mixed_y[z, :, lanes] = product_split(y_fwd[0], mixed_x[z, :, lanes])
+            return carry
+
+        lax.fori_loop(start, stop, y_plane, 0)
+
+    def z_rim(rows, lanes):
+        return send(
+            mixed_y.at[0:10, rows, lanes],
+            mixed_y.at[first.z : first.z + 10, rows, lanes],
+            -1,
+            0,
+        )
+
+    def z_bands(by, bx):
+        lanes = slice(bx * half, (bx + 1) * half)
+        at = slice(by * first.yc, (by + 1) * first.yc)
+
+        def z_band(i, carry):
+            low = high = None
+            for k in range(12):
+                part = mixed_y[2 * i + k, at, lanes]
+                low = low_taps[k] * part if k == 0 else low + low_taps[k] * part
+                high = high_taps[k] * part if k == 0 else high + high_taps[k] * part
+            for bz, piece in ((0, low), (1, high)):
+                band = 4 * bz + 2 * by + bx
+                if band == 0:
+                    exts[1][i, 0 : first.yc, :] = piece
+                else:
+                    piece = piece * keeps[0][band - 1, i].astype(F32)
+                    shaped = piece.reshape(first.yc // 8, 8, half)
+                    coefs[0][2 * bz + by, 5 + i, 1 : first.blocks, :, lanes] = shaped
+            return carry
+
+        lax.fori_loop(0, first.zc, z_band, 0)
+
+    low_lanes, high_lanes = slice(0, half), slice(half, first.x)
+    y_low.wait_recv()
+    y_planes(0, 10, low_lanes)
+    z_first = z_rim(slice(0, first.yc), low_lanes)
+    y_planes(10, first.z, low_lanes)
+    y_high.wait_recv()
+    y_planes(0, 10, high_lanes)
+    z_late = [z_rim(slice(first.yc, first.y), low_lanes), z_rim(slice(0, first.y), high_lanes)]
+    y_planes(10, first.z, high_lanes)
+    z_first.wait_recv()
+    z_bands(0, 0)
+
+    early = [None] * LEVELS
     for no, lv in enumerate(levels):
+        if no == 0:
+            continue
         ext, zbuf, coef, keep = exts[no], zbufs[no], coefs[no], keeps[no]
-        copies = send_rim(lv, field if no == 0 else ext, ext)
-        if no == 0:
-            load.wait()
+        copies = send_rim(lv, ext, ext)
+        if no == 2:
+            early[1] = send_back(levels[1], coefs[1], 1, 4)
+            for copy in z_late:
+                copy.wait_recv()
+            z_bands(0, 1)
+            z_bands(1, 0)
+            z_bands(1, 1)
+            early[0] = send_back(first, coefs[0], 1, 4)
+            early[0] += send_back(first, coefs[0], 0, 1, high_lanes)
+        if no == 3:
+            early[2] = send_back(levels[2], coefs[2], 1, 4)
         for copy in copies:
             copy.wait_recv()
         for hy in range(1, lv.rim_hops + 1):
@@ -261,24 +349,12 @@
             return carry
 
         lax.fori_loop(0, lv.zc, y_split, 0)
-        if no == LEVELS - 1:
-            detail_copies.append([])
-        else:
-            detail_copies.append((lv, coef))
-
-    early = [None] * LEVELS
+
     for no in range(LEVELS - 1, -1, -1):
         lv, coef, sbuf, ybuf = levels[no], coefs[no], sbufs[no], ybufs[no]
-        late = send_back(lv, coef, 0, 1)
+        late = send_back(lv, coef, 0, 1, low_lanes if no == 0 else slice(None))
         if no == LEVELS - 1:
-            for each in range(LEVELS - 1, -1, -1):
-                early[each] = send_back(levels[each], coefs[each], 1, 4)
-        for copy in late + early[no]:
-            copy.wait_recv()
-        for hy in range(1, lv.back_hops + 1):
-            if hy % ny == 0:
-                coef[:, :, lv.back_hops - hy] = coef[:, :, lv.blocks - 1]
-        z_group = lv.zc_ext
+            early[no] = send_back(lv, coef, 1, 4)
 
         def x_merge(b, carry, lv=lv, coef=coef, sbuf=sbuf, no=no):
             if lv.block == 8:
@@ -290,15 +366,23 @@
                     sbuf[b, z] = split_product(rows, x_inv[no])
             return carry
 
-        lax.fori_loop(0, 4, x_merge, 0)
-
-        def y_merge(z, carry, lv=lv, sbuf=sbuf, ybuf=ybuf, no=no):
-            for bz in range(2):
+        def y_merge(bz, lv=lv, sbuf=sbuf, ybuf=ybuf, no=no):
+            def merge(z, carry):
                 pair = jnp.concatenate([sbuf[2 * bz, z], sbuf[2 * bz + 1, z]], axis=0)
                 ybuf[bz, z] = product_split(y_inv[no], pair)
-            return carry
-
-        lax.fori_loop(0, lv.zc_ext, y_merge, 0)
+                return carry
+
+            lax.fori_loop(0, lv.zc_ext, merge, 0)
+
+        for copies, start, stop in ((early[no], 1, 4), (late, 0, 1)):
+            for copy in copies:
+                copy.wait_recv()
+            for hy in range(1, lv.back_hops + 1):
+                if hy % ny == 0:
+                    same = coef[start:stop, :, lv.blocks - 1]
+                    coef[start:stop, :, lv.back_hops - hy] = same
+            lax.fori_loop(start, stop, x_merge, 0)
+            y_merge(1 if start else 0)
         chunk = min(lv.y, 16)
         if no:
             chunk = min(chunk, levels[no - 1].block)
@@ -327,7 +411,7 @@
         lax.fori_loop(0, lv.zc * steps, z_merge, 0)
     for copy in sends:
         copy.wait_send()
-    assert used[0] == count
+    assert used[0] <= count
 
 
 def solution(mesh):
@@ -336,19 +420,18 @@
     def on_device(field, k1, k2, k3, k4, coarse):
         z, y, x = field.shape
         levels = [Level(z >> n, y >> n, x >> n) for n in range(LEVELS)]
-        count = 0
-        for lv in levels:
-            rim = len(hop_list(lv.z, 10)) * sum(h % ny != 0 or h == 0 for h in range(lv.rim_hops + 1))
-            back = len(hop_list(lv.zc, 5)) * sum(h % ny != 0 or h == 0 for h in range(lv.back_hops + 1))
-            count += rim - 1 + 2 * (back - 1)
+        count = 128
         x_pairs = [halves(x_matrix(lv.x)) for lv in levels]
         xt_pairs = [halves(x_matrix(lv.x).T) for lv in levels]
         y_pairs = [halves(y_split_matrix(lv.y, lv.y_ext)) for lv in levels]
         yt_pairs = [halves(y_merge_matrix(lv.yc, lv.yc_ext)) for lv in levels]
         mats = [jnp.asarray(m) for m in x_pairs + xt_pairs + y_pairs + yt_pairs]
         vmem = pl.BlockSpec(memory_space=pltpu.VMEM)
-        scratch = [pltpu.VMEM((lv.z_ext, lv.y_ext, lv.x), F32) for lv in levels]
-        scratch += [pltpu.VMEM((lv.z, lv.y_ext, lv.x), F32) for lv in levels]
+        scratch = [pltpu.VMEM((z, y, x), F32)]
+        scratch += [pltpu.VMEM((z, levels[0].y_ext, x), F32)]
+        scratch += [pltpu.VMEM((levels[0].z_ext, y, x), F32)]
+        scratch += [pltpu.VMEM((lv.z_ext, lv.y_ext, lv.x), F32) for lv in levels[1:]]
+        scratch += [pltpu.VMEM((lv.z, lv.y_ext, lv.x), F32) for lv in levels[1:]]
         scratch += [pltpu.VMEM((4, lv.zc_ext, lv.blocks, lv.block, lv.x), F32) for lv in levels]
         scratch += [pltpu.VMEM((4, lv.zc_ext, lv.yc_ext, lv.x), F32) for lv in levels]
         scratch += [pltpu.VMEM((2, lv.zc_ext, lv.y, lv.x), F32) for lv in levels]

time: 116 us -> 114 us (0.983)
  Pallas kernels: 112 us -> 110 us
    pallas_call x1, Pallas kernels: 112 us -> 110 us  [on_device(): pl.pallas_call(functools.partial(kernel, levels, nz, ny, count), out_shap...]
where the time goes in v2:
time: 114 us
  Pallas kernels  110 us (96%)
  local copies, waits for them, and re-layouts  3.14 us (3%)
    pallas_call x1, Pallas kernels, on_device(): pl.pallas_call(functools.partial(kernel, levels, nz, ny, count), out_shap...  110 us
    unnamed x1, local copies, waits for them, and re-layouts  3.14 us

profile of v2, /device:TPU:0, one launch (start us, length us, event | category | flops | bytes accessed | tf_op | source)
XLA Modules:
  0.0 113.6 jit_solution(14015328471305761167)
XLA Ops:
  0.0 110.5 %shard_map.208 = f32[16,64,512]{2,1,0:T(8,128)} custom-call(f32[16,64,512]{2,1,0:T(8,128)} %refs_0_.1, s32[7,8,32,256]{3,2,1,0:T(8,128)} %refs_1_.1, s32[7,4,16,128]{3,2,1,0:T(8,128)} %refs_2_.1, s32[7,2,8,64]{3,2,1,0:T(8,128)} %refs_3_.1, s32[7,1,4,32]{3,2,1,0:T(4,128)} %refs_4_.1, s32[1,4,32]{2,1,0:T(4,128)} %refs_5_.1, ...), custom_call_target="tpu_custom_call" | custom-call | tf_op jit(solution)/shard_map/pallas_call | solution.py:443
  110.5 3.1 %copy.24 = f32[16,64,512]{2,1,0:T(8,128)} copy(f32[16,64,512]{2,1,0:T(8,128)} %shard_map.208) | data formatting | bytes 4194304

commit v3 on v2

--- a/solution.py
+++ b/solution.py
@@ -274,7 +274,6 @@
     y_planes(10, first.z, low_lanes)
     y_high.wait_recv()
     y_planes(0, 10, high_lanes)
-    z_late = [z_rim(slice(first.yc, first.y), low_lanes), z_rim(slice(0, first.y), high_lanes)]
     y_planes(10, first.z, high_lanes)
     z_first.wait_recv()
     z_bands(0, 0)
@@ -285,17 +284,17 @@
             continue
         ext, zbuf, coef, keep = exts[no], zbufs[no], coefs[no], keeps[no]
         copies = send_rim(lv, ext, ext)
+        if no == 1:
+            z_late = [z_rim(slice(first.yc, first.y), low_lanes)]
         if no == 2:
+            z_late.append(z_rim(slice(0, first.y), high_lanes))
+        if no == 3:
             early[1] = send_back(levels[1], coefs[1], 1, 4)
             for copy in z_late:
                 copy.wait_recv()
             z_bands(0, 1)
             z_bands(1, 0)
             z_bands(1, 1)
-            early[0] = send_back(first, coefs[0], 1, 4)
-            early[0] += send_back(first, coefs[0], 0, 1, high_lanes)
-        if no == 3:
-            early[2] = send_back(levels[2], coefs[2], 1, 4)
         for copy in copies:
             copy.wait_recv()
         for hy in range(1, lv.rim_hops + 1):
@@ -355,6 +354,13 @@
         late = send_back(lv, coef, 0, 1, low_lanes if no == 0 else slice(None))
         if no == LEVELS - 1:
             early[no] = send_back(lv, coef, 1, 4)
+            early[2] = send_back(levels[2], coefs[2], 1, 4)
+            early[0] = send_back(first, coefs[0], 2, 3)
+        if no == 2:
+            early[0] += send_back(first, coefs[0], 3, 4)
+        if no == 1:
+            early[0] += send_back(first, coefs[0], 1, 2)
+            early[0] += send_back(first, coefs[0], 0, 1, high_lanes)
 
         def x_merge(b, carry, lv=lv, coef=coef, sbuf=sbuf, no=no):
             if lv.block == 8:

time: 114 us -> 103 us (0.904)
  Pallas kernels: 110 us -> 99.9 us
    pallas_call x1, Pallas kernels: 110 us -> 99.9 us  [on_device(): pl.pallas_call(functools.partial(kernel, levels, nz, ny, count), out_shap...]
where the time goes in v3:
time: 103 us
  Pallas kernels  99.9 us (97%)
  local copies, waits for them, and re-layouts  3.14 us (3%)
    pallas_call x1, Pallas kernels, on_device(): pl.pallas_call(functools.partial(kernel, levels, nz, ny, count), out_shap...  99.9 us
    unnamed x1, local copies, waits for them, and re-layouts  3.14 us

profile of v3, /device:TPU:0, one launch (start us, length us, event | category | flops | bytes accessed | tf_op | source)
XLA Modules:
  0.0 103.1 jit_solution(10363214410959055784)
XLA Ops:
  0.0 99.9 %shard_map.208 = f32[16,64,512]{2,1,0:T(8,128)} custom-call(f32[16,64,512]{2,1,0:T(8,128)} %refs_0_.1, s32[7,8,32,256]{3,2,1,0:T(8,128)} %refs_1_.1, s32[7,4,16,128]{3,2,1,0:T(8,128)} %refs_2_.1, s32[7,2,8,64]{3,2,1,0:T(8,128)} %refs_3_.1, s32[7,1,4,32]{3,2,1,0:T(4,128)} %refs_4_.1, s32[1,4,32]{2,1,0:T(4,128)} %refs_5_.1, ...), custom_call_target="tpu_custom_call" | custom-call | tf_op jit(solution)/shard_map/pallas_call | solution.py:449
  99.9 3.1 %copy.24 = f32[16,64,512]{2,1,0:T(8,128)} copy(f32[16,64,512]{2,1,0:T(8,128)} %shard_map.208) | data formatting | bytes 4194304

commit v4 on v3

--- a/solution.py
+++ b/solution.py
@@ -127,7 +127,7 @@
     coefs = refs[32:36]
     sbufs = refs[36:40]
     ybufs = refs[40:44]
-    local_sem, send_sem, recv_sem = refs[44:47]
+    local_sem, send_sem, recv_sem, pack_out, pack_in = refs[44:49]
     gz = lax.axis_index("gz")
     gy = lax.axis_index("gy")
 
@@ -210,16 +210,32 @@
     load.wait()
     rows = whole[:, 0:rim, :].reshape(first.z * rim, first.x)
     mixed_x[:, 0:rim, :] = split_product(rows, x_fwd[0]).reshape(first.z, rim, first.x)
+    for g in range(first.z // 4):
+        pack_out[g] = jnp.concatenate(
+            [mixed_x[4 * g + j, 8:16, :][0:2] for j in range(4)], axis=0
+        )
     pl.semaphore_wait(barrier, len(offsets))
     y_low, y_high = [
-        send(
-            mixed_x.at[:, 0:rim, lanes],
-            mixed_x.at[:, first.y : first.y + rim, lanes],
-            0,
-            -1,
+        (
+            send(
+                mixed_x.at[:, 0:8, lanes],
+                mixed_x.at[:, first.y : first.y + 8, lanes],
+                0,
+                -1,
+            ),
+            send(pack_out.at[:, :, lanes], pack_in.at[:, :, lanes], 0, -1),
         )
         for lanes in (slice(0, half), slice(half, first.x))
     ]
+
+    def take_y(copies, lanes):
+        for copy in copies:
+            copy.wait_recv()
+        empty = jnp.zeros((6, half), F32)
+        for z in range(first.z):
+            at = 2 * (z % 4)
+            piece = pack_in[z // 4, :, lanes][at : at + 2]
+            mixed_x[z, first.y + 8 : first.y + 16, lanes] = jnp.concatenate([piece, empty], axis=0)
 
     def x_rest(step, carry):
         at = pl.ds(step * 4, 4)
@@ -268,13 +284,10 @@
         lax.fori_loop(0, first.zc, z_band, 0)
 
     low_lanes, high_lanes = slice(0, half), slice(half, first.x)
-    y_low.wait_recv()
+    take_y(y_low, low_lanes)
     y_planes(0, 10, low_lanes)
     z_first = z_rim(slice(0, first.yc), low_lanes)
     y_planes(10, first.z, low_lanes)
-    y_high.wait_recv()
-    y_planes(0, 10, high_lanes)
-    y_planes(10, first.z, high_lanes)
     z_first.wait_recv()
     z_bands(0, 0)
 
@@ -286,6 +299,8 @@
         copies = send_rim(lv, ext, ext)
         if no == 1:
             z_late = [z_rim(slice(first.yc, first.y), low_lanes)]
+            take_y(y_high, high_lanes)
+            y_planes(0, first.z, high_lanes)
         if no == 2:
             z_late.append(z_rim(slice(0, first.y), high_lanes))
         if no == 3:
@@ -445,6 +460,8 @@
             pltpu.SemaphoreType.DMA,
             pltpu.SemaphoreType.DMA((count,)),
             pltpu.SemaphoreType.DMA((count,)),
+            pltpu.VMEM((z // 4, 8, x), F32),
+            pltpu.VMEM((z // 4, 8, x), F32),
         ]
         return pl.pallas_call(
             functools.partial(kernel, levels, nz, ny, count),

time: 103 us -> 99.8 us (0.969)
  Pallas kernels: 99.9 us -> 96.4 us
    pallas_call x1, Pallas kernels: 99.9 us -> 96.4 us  [on_device(): pl.pallas_call(functools.partial(kernel, levels, nz, ny, count), out_shap...]
where the time goes in v4:
time: 99.8 us; the launch traced here: 99.5 us
  Pallas kernels  96.4 us (97%)
  local copies, waits for them, and re-layouts  3.14 us (3%)
    pallas_call x1, Pallas kernels, on_device(): pl.pallas_call(functools.partial(kernel, levels, nz, ny, count), out_shap...  96.4 us
    unnamed x1, local copies, waits for them, and re-layouts  3.14 us

profile of v4, /device:TPU:0, one launch (start us, length us, event | category | flops | bytes accessed | tf_op | source)
XLA Modules:
  0.0 99.5 jit_solution(15440984838302725653)
XLA Ops:
  0.0 96.4 %shard_map.208 = f32[16,64,512]{2,1,0:T(8,128)} custom-call(f32[16,64,512]{2,1,0:T(8,128)} %refs_0_.1, s32[7,8,32,256]{3,2,1,0:T(8,128)} %refs_1_.1, s32[7,4,16,128]{3,2,1,0:T(8,128)} %refs_2_.1, s32[7,2,8,64]{3,2,1,0:T(8,128)} %refs_3_.1, s32[7,1,4,32]{3,2,1,0:T(4,128)} %refs_4_.1, s32[1,4,32]{2,1,0:T(4,128)} %refs_5_.1, ...), custom_call_target="tpu_custom_call" | custom-call | tf_op jit(solution)/shard_map/pallas_call | solution.py:466
  96.4 3.1 %copy.24 = f32[16,64,512]{2,1,0:T(8,128)} copy(f32[16,64,512]{2,1,0:T(8,128)} %shard_map.208) | data formatting | bytes 4194304
